TPU v7x, 32 devices: a whole 2x2x4 slice. The times are simulated.
32 devices in a mesh: dp: 4 (over y, x), mp: 8 (over z, core).
Axes of the slice: x: 2, y: 2, z: 4, core: 2. Of those that a mesh axis runs over, the one named last changes fastest.
Arguments:
- hidden_in: bfloat16 [256, 8192], P(('dp', 'mp')), may hold values from -6 to 6
- out_grad: bfloat16 [256, 8192], P(('dp', 'mp')), may hold values from -6 to 6
- gate_pre: bfloat16 [256, 28672], P('dp', 'mp'), may hold values from -8 to 8
- up_pre: bfloat16 [256, 28672], P('dp', 'mp'), may hold values from -6 to 6
- down_weight: bfloat16 [28672, 8192], P('mp', 'dp'), may hold values from -0.03125 to 0.03125
- proj_in: bfloat16 [64, 8192], replicated, may hold values from -0.0625 to 0.0625
- proj_grad: bfloat16 [64, 8192], replicated, may hold values from -0.0625 to 0.0625
- proj_hidden: bfloat16 [64, 28672], P(None, 'mp'), may hold values from -0.03125 to 0.03125
- proj_gate: bfloat16 [64, 28672], P(None, 'mp'), may hold values from -0.0625 to 0.0625
- proj_up: bfloat16 [64, 28672], P(None, 'mp'), may hold values from -0.0625 to 0.0625
- doc_lengths: int32 [4, 8], P('dp'), may hold values from 1 to 32, 64 in all within a row
Outputs:
- gate_grad: bfloat16 [256, 28672], P('dp', 'mp')
- up_grad: bfloat16 [256, 28672], P('dp', 'mp')
- sketches: float32 [4, 1536, 64], P('dp', 'mp')
Inputs may be any that keep to these rules, and one draw needn't show every extreme that they name: `doc_lengths`: each row holds 8 document lengths, each 1 or more, summing to 64; in every row the largest is exactly 32.
All inputs are finite; a program needn't handle non-finite values.
Results may differ from a plain program's by a relative error of at most 0.0028.
Values may be sent and summed in bfloat16 or wider, within the bound.
A program may use at most 128 MiB of HBM per device.

v0:
```python
import jax
import jax.numpy as jnp
from jax import lax
from jax.sharding import PartitionSpec as P


def sketch_of(member, first_side, second_side):
    masked = (member[:, :, None] * first_side[:, None, :]).reshape(first_side.shape[0], -1)
    return jnp.dot(masked.T, second_side, precision=lax.Precision.HIGHEST)


def membership(positions, doc_sizes):
    starts = jnp.cumsum(doc_sizes) - doc_sizes
    return (
        (positions[:, None] >= starts[None, :])
        & (positions[:, None] < (starts + doc_sizes)[None, :])
    ).astype(jnp.float32)


def local(
    hidden_in,
    out_grad,
    gate_pre,
    up_pre,
    down_weight,
    proj_in,
    proj_grad,
    proj_hidden,
    proj_gate,
    proj_up,
    doc_lengths,
):
    own_rows = hidden_in.shape[0]
    weight_full = lax.all_gather(down_weight, "dp", axis=1, tiled=True)
    grad_hidden = lax.dot_general(
        lax.all_gather(out_grad, "mp", axis=0, tiled=True),
        weight_full,
        (((1,), (1,)), ((), ())),
        preferred_element_type=jnp.float32,
    )
    gate_value = gate_pre.astype(jnp.float32)
    up_value = up_pre.astype(jnp.float32)
    sigmoid_gate = jax.nn.sigmoid(gate_value)
    silu_gate = gate_value * sigmoid_gate
    hidden = (silu_gate * up_value).astype(jnp.bfloat16)
    gate_grad = (
        grad_hidden * up_value * sigmoid_gate * (1.0 + gate_value * (1.0 - sigmoid_gate))
    ).astype(jnp.bfloat16)
    up_grad = (grad_hidden * silu_gate).astype(jnp.bfloat16)
    hidden_side = jnp.dot(hidden, proj_hidden.T, preferred_element_type=jnp.float32)
    gate_side = jnp.dot(gate_grad, proj_gate.T, preferred_element_type=jnp.float32)
    up_side = jnp.dot(up_grad, proj_up.T, preferred_element_type=jnp.float32)
    grad_side = jnp.dot(out_grad, proj_grad.T, preferred_element_type=jnp.float32)
    input_side = jnp.dot(hidden_in, proj_in.T, preferred_element_type=jnp.float32)
    doc_sizes = doc_lengths[0]
    rank_size = hidden_side.shape[1]
    stacked = jnp.concatenate([hidden_side, gate_side, up_side], axis=1)
    own_sides = lax.psum_scatter(stacked, "mp", scatter_dimension=0, tiled=True)
    offset = lax.axis_index("mp") * own_rows
    member = membership(offset + jnp.arange(own_rows, dtype=jnp.int32), doc_sizes)
    partial_sketch = jnp.concatenate(
        [
            sketch_of(member, own_sides[:, :rank_size], grad_side),
            sketch_of(member, input_side, own_sides[:, rank_size : 2 * rank_size]),
            sketch_of(member, input_side, own_sides[:, 2 * rank_size :]),
        ],
        axis=0,
    )
    sketches = lax.psum_scatter(partial_sketch, "mp", scatter_dimension=0, tiled=True)
    return (gate_grad, up_grad, sketches[None])


def solution(mesh):
    placed = (
        P(("dp", "mp"), None),
        P(("dp", "mp"), None),
        P("dp", "mp"),
        P("dp", "mp"),
        P("mp", "dp"),
        P(),
        P(),
        P(None, "mp"),
        P(None, "mp"),
        P(None, "mp"),
        P("dp", None),
    )
    return jax.shard_map(
        local,
        mesh=mesh,
        in_specs=placed,
        out_specs=(P("dp", "mp"), P("dp", "mp"), P("dp", "mp", None)),
        check_vma=False,
    )
```

profile of v0, /device:TPU:0, one launch (start us, length us, event | category | flops | bytes accessed | tf_op | source)
XLA Modules:
  0.0 642.8 jit_solution(12306726890652725986)
XLA Ops:
  7.2 0.7 all-gather.3.cloned.1.call-update
  8.0 0.7 all-gather.5.cloned.1.call-update
  8.7 0.8 reduce-window.4
  9.6 0.7 fusion.14
  10.2 1.3 fusion.18
  11.5 1.7 fusion.20
  13.2 1.7 fusion.8
  14.9 19.7 %all-gather.3.cloned.1.call-done = bf16[64,8192]{1,0:T(8,128)(2,1)} async-done(((bf16[8,8192]{1,0:T(8,128)(2,1)}), bf16[64,8192]{1,0:T(8,128)(2,1)}) %all-gather.3.cloned.1.call-update) | async-done | bytes 1048592 | tf_op jit(solution)/shard_map/all_gather | solution.py:36
  34.6 508.7 %all-gather.5.cloned.1.call-done = bf16[3584,8192]{1,0:T(8,128)(2,1)} async-done(((bf16[3584,2048]{1,0:T(8,128)(2,1)}), bf16[3584,8192]{1,0:T(8,128)(2,1)}) %all-gather.5.cloned.1.call-update) | async-done | bytes 58720272 | tf_op jit(solution)/shard_map/all_gather | solution.py:34
  543.3 24.7 %multiply_convert_fusion = (bf16[64,3584]{1,0:T(8,128)(2,1)S(1)}, bf16[64,3584]{1,0:T(8,128)(2,1)S(1)}) fusion(bf16[64,3584]{1,0:T(8,128)(2,1)} %param.13, bf16[64,3584]{1,0:T(8,128)(2,1)} %param.14, bf16[64,8192]{1,0:T(8,128)(2,1)} %all-gather.3.cloned.1.call-done, bf16[3584,8192]{1,0:T(8,128)(2,1)} %all-gather.5.cloned.1.call-done), kind=kOutput, calls=%fused_computation.13 | convolution fusion | flops 3761537024 | bytes 61603840 | tf_op jit(solution)/shard_map/dot_general | solution.py:35
  568.0 0.3 fusion.16
  568.3 0.3 fusion.17
  568.6 0.7 pad_maximum_fusion.1
  569.5 30.5 %reduce-scatter.5.cloned.1.call-done = f32[8,192]{1,0:T(8,128)} async-done(((f32[64,192]{1,0:T(8,128)}), f32[8,192]{1,0:T(8,128)}) %reduce-scatter.5.cloned.1.call-update) | async-done | bytes 6160 | tf_op jit(solution)/shard_map/reduce_scatter | solution.py:58
  600.0 0.7 slice.12
  600.6 0.1 broadcast_multiply_fusion.1
  600.7 0.1 mul.77
  600.8 0.1 mul.74
  600.9 0.3 fusion.19
  601.2 1.1 fusion.12
  602.3 1.0 fusion.10
  603.3 1.2 copy.14
  604.5 30.1 %reduce-scatter.7.cloned.1.call-done = f32[192,64]{1,0:T(8,128)} async-done(((f32[1536,64]{1,0:T(8,128)}), f32[192,64]{1,0:T(8,128)}) %reduce-scatter.7.cloned.1.call-update) | async-done | bytes 49168
  634.6 1.6 copy.15
  (19 shorter events, 0.3 us)
Async XLA Ops:
  7.2 3.1 copy-start
  7.2 560.9 %copy-start.3 = (bf16[64,3584]{1,0:T(8,128)(2,1)S(1)}, bf16[64,3584]{1,0:T(8,128)(2,1)}, u32[]{:S(2)}) copy-start(bf16[64,3584]{1,0:T(8,128)(2,1)} %param.19) | copy-start | bytes 1376260
  7.2 561.1 %copy-start.4 = (bf16[64,3584]{1,0:T(8,128)(2,1)S(1)}, bf16[64,3584]{1,0:T(8,128)(2,1)}, u32[]{:S(2)}) copy-start(bf16[64,3584]{1,0:T(8,128)(2,1)} %param.20) | copy-start | bytes 1376260
  7.2 27.4 %all-gather.3.cloned.1.call-start = ((), (), s32[]{:S(2)}) async-start(), calls=%async_computation.2 | async-start | bytes 1179648 | tf_op jit(solution)/shard_map/all_gather | solution.py:36
  7.9 535.3 %all-gather.5.cloned.1.call-start = ((), (), s32[]{:S(2)}) async-start(), calls=%async_computation.3 | async-start | bytes 73400320 | tf_op jit(solution)/shard_map/all_gather | solution.py:34
  8.7 591.3 %reduce-scatter.5.cloned.1.call-start = ((), (), s32[]{:S(2)}) async-start(), calls=%async_computation.4 | async-start | bytes 73728 | tf_op jit(solution)/shard_map/reduce_scatter | solution.py:58
  568.0 68.2 %copy-start.1 = (bf16[64,3584]{1,0:T(8,128)(2,1)}, bf16[64,3584]{1,0:T(8,128)(2,1)S(1)}, u32[]{:S(2)}) copy-start(bf16[64,3584]{1,0:T(8,128)(2,1)S(1)} %get-tuple-element.3) | copy-start | bytes 1376260
  568.0 68.2 %copy-start.2 = (bf16[64,3584]{1,0:T(8,128)(2,1)}, bf16[64,3584]{1,0:T(8,128)(2,1)S(1)}, u32[]{:S(2)}) copy-start(bf16[64,3584]{1,0:T(8,128)(2,1)S(1)} %get-tuple-element.4) | copy-start | bytes 1376260
  569.3 65.3 %reduce-scatter.7.cloned.1.call-start = ((), (), s32[]{:S(2)}) async-start(), calls=%async_computation.5 | async-start | bytes 884736
Sparse Core Ops, SparseCore 0:
  9.6 24.9 all-gather.2
  36.5 506.7 all-gather.4
  569.5 30.4 reduce-scatter.4
  604.6 29.9 reduce-scatter.6
where the time goes:
time: 643 us
  waiting for transfers between devices  590 us (92%)
  matrix products  32.3 us (5%)
  between operations  13.9 us (2%)
    all_gather x1, waiting for transfers between devices, local(): weight_full = lax.all_gather(down_weight, 'dp', axis=1, tiled=True)  509 us
    unnamed x5, waiting for transfers between devices  31.6 us
    reduce_scatter x1, waiting for transfers between devices, local(): own_sides = lax.psum_scatter(stacked, 'mp', scatter_dimension=0, tiled=True)  30.5 us
    dot_general x1, matrix products, local(): lax.dot_general(lax.all_gather(out_grad, 'mp', axis=0, tiled=True), weigh...  24.7 us
    all_gather x1, waiting for transfers between devices, local(): lax.all_gather(out_grad, 'mp', axis=0, tiled=True)  19.7 us
  transfers between devices with their start and end apart: 4, of which 4 were waited for; matrix products, arithmetic and copies ran while one was open for 1% of the time, Pallas kernels for 0%

commit v1 on v0

v1 whole, which is shorter than its diff:
```python
import jax
import jax.numpy as jnp
from jax import lax
from jax.sharding import PartitionSpec as P


def own_sketch_rows(sides, doc_sizes, rank, row_count):
    hidden, gate, up, grad, inp = [sides[:, s * rank : (s + 1) * rank] for s in range(5)]
    firsts = jnp.concatenate([hidden, inp, inp], axis=1)
    seconds = jnp.concatenate([grad, gate, up], axis=1)
    docs = doc_sizes.shape[0]
    r = lax.axis_index("mp") * row_count + jnp.arange(row_count, dtype=jnp.int32)
    which, doc, lane = r // (docs * rank), (r // rank) % docs, r % rank
    pick = (jnp.arange(3 * rank)[:, None] == (which * rank + lane)[None, :]).astype(jnp.float32)
    chosen = jnp.dot(firsts, pick, precision=lax.Precision.HIGHEST)
    ends = jnp.cumsum(doc_sizes)
    of_doc = doc[None, :] == jnp.arange(docs)[:, None]
    end = jnp.sum(jnp.where(of_doc, ends[:, None], 0), axis=0)
    start = jnp.sum(jnp.where(of_doc, (ends - doc_sizes)[:, None], 0), axis=0)
    t = jnp.arange(sides.shape[0], dtype=jnp.int32)[:, None]
    masked = jnp.where((t >= start[None, :]) & (t < end[None, :]), chosen, 0.0)
    full = jnp.dot(masked.T, seconds, precision=lax.Precision.HIGHEST)
    out = jnp.zeros((row_count, rank), jnp.float32)
    for w in range(3):
        out = out + jnp.where((which == w)[:, None], full[:, w * rank : (w + 1) * rank], 0.0)
    return out


def local(
    hidden_in,
    out_grad,
    gate_pre,
    up_pre,
    down_weight,
    proj_in,
    proj_grad,
    proj_hidden,
    proj_gate,
    proj_up,
    doc_lengths,
):
    n_dp, n_mp = lax.axis_size("dp"), lax.axis_size("mp")
    own_rows, rank = hidden_in.shape[0], proj_in.shape[0]
    pack, units = gate_pre.shape
    me = lax.axis_index("dp")
    turned = lax.all_to_all(out_grad, "dp", split_axis=1, concat_axis=0, tiled=True)
    gathered = lax.all_gather(turned.reshape(n_dp, own_rows, -1), "mp", axis=1)
    gathered = gathered.reshape(n_dp * pack, -1)
    partial = lax.dot_general(
        gathered, down_weight, (((1,), (1,)), ((), ())), preferred_element_type=jnp.float32
    ).reshape(n_dp, pack, units)
    arrived = lax.all_to_all(
        partial.astype(jnp.bfloat16), "dp", split_axis=0, concat_axis=0, tiled=True
    )
    own = lax.dynamic_index_in_dim(partial, me, 0, keepdims=False)
    others = jnp.where(
        (jnp.arange(n_dp) == me)[:, None, None], 0.0, arrived.astype(jnp.float32)
    )
    grad_hidden = own + jnp.sum(others, axis=0)
    gate_value = gate_pre.astype(jnp.float32)
    up_value = up_pre.astype(jnp.float32)
    sigmoid_gate = jax.nn.sigmoid(gate_value)
    silu_gate = gate_value * sigmoid_gate
    hidden = (silu_gate * up_value).astype(jnp.bfloat16)
    gate_grad = (
        grad_hidden * up_value * sigmoid_gate * (1.0 + gate_value * (1.0 - sigmoid_gate))
    ).astype(jnp.bfloat16)
    up_grad = (grad_hidden * silu_gate).astype(jnp.bfloat16)
    hidden_side = jnp.dot(hidden, proj_hidden.T, preferred_element_type=jnp.float32)
    gate_side = jnp.dot(gate_grad, proj_gate.T, preferred_element_type=jnp.float32)
    up_side = jnp.dot(up_grad, proj_up.T, preferred_element_type=jnp.float32)
    grad_side = jnp.dot(out_grad, proj_grad.T, preferred_element_type=jnp.float32)
    input_side = jnp.dot(hidden_in, proj_in.T, preferred_element_type=jnp.float32)
    stacked = jnp.concatenate([hidden_side, gate_side, up_side], axis=1)
    own_sides = lax.psum_scatter(stacked, "mp", scatter_dimension=0, tiled=True)
    sides = lax.all_gather(
        jnp.concatenate([own_sides, grad_side, input_side], axis=1), "mp", axis=0, tiled=True
    )
    docs = doc_lengths.shape[1]
    sketches = own_sketch_rows(sides, doc_lengths[0], rank, 3 * docs * rank // n_mp)
    return (gate_grad, up_grad, sketches[None])


def solution(mesh):
    placed = (
        P(("dp", "mp"), None),
        P(("dp", "mp"), None),
        P("dp", "mp"),
        P("dp", "mp"),
        P("mp", "dp"),
        P(),
        P(),
        P(None, "mp"),
        P(None, "mp"),
        P(None, "mp"),
        P("dp", None),
    )
    return jax.shard_map(
        local,
        mesh=mesh,
        in_specs=placed,
        out_specs=(P("dp", "mp"), P("dp", "mp"), P("dp", "mp", None)),
        check_vma=False,
    )
```

time: 643 us -> 135 us (0.21)
  waiting for transfers between devices: 590 us -> 70.3 us
  blocking collectives: 0 us -> 24.4 us
  matrix products: 32.3 us -> 16.7 us
    all_gather x2 -> x1, waiting for transfers between devices: 528 us -> 22.3 us  [local(): gathered = lax.all_gather(turned.reshape(n_dp, own_rows, -1), 'mp', axis=1)]
    unnamed x5 -> x2, waiting for transfers between devices: 31.6 us -> 0.03 us
    all_to_all x0 -> x1, waiting for transfers between devices: none -> 18.6 us  [local(): lax.all_to_all(partial.astype(jnp.bfloat16), 'dp', split_axis=0, concat_a...]
    dot_general x4 -> x3, matrix products: 27.1 us -> 12.6 us  [the longest x1 11.9 us: local(): lax.dot_general(gathered, down_weight, (((1,), (1,)), ((), ())), preferre...]
    all_gather x0 -> x1, blocking collectives: none -> 13.9 us  [local(): lax.all_gather(jnp.concatenate([own_sides, grad_side, input_side], axis=1...]
    all_to_all x0 -> x1, blocking collectives: none -> 10.5 us  [local(): lax.all_to_all(out_grad, 'dp', split_axis=1, concat_axis=0, tiled=True)]
  transfers between devices with their start and end apart: 4 -> 3, of which waited for: 4 -> 3; matrix products, arithmetic and copies ran while one was open for 1% -> 3% of each run, Pallas kernels for 0% -> 0%
where the time goes in v1:
time: 135 us; the launch traced here: 134 us
  waiting for transfers between devices  70.3 us (52%)
  blocking collectives  24.4 us (18%)
  matrix products  16.7 us (12%)
  between operations  14.2 us (11%)
  other arithmetic  4.86 us (4%)
  starting transfers between devices  3.83 us (3%)
    reduce_scatter x1, waiting for transfers between devices, local(): own_sides = lax.psum_scatter(stacked, 'mp', scatter_dimension=0, tiled=True)  29.4 us
    all_gather x1, waiting for transfers between devices, local(): gathered = lax.all_gather(turned.reshape(n_dp, own_rows, -1), 'mp', axis=1)  22.3 us
    all_to_all x1, waiting for transfers between devices, local(): lax.all_to_all(partial.astype(jnp.bfloat16), 'dp', split_axis=0, concat_a...  18.6 us
    all_gather x1, blocking collectives, local(): lax.all_gather(jnp.concatenate([own_sides, grad_side, input_side], axis=1...  13.9 us
    dot_general x1, matrix products, local(): lax.dot_general(gathered, down_weight, (((1,), (1,)), ((), ())), preferre...  11.9 us
    all_to_all x1, blocking collectives, local(): lax.all_to_all(out_grad, 'dp', split_axis=1, concat_axis=0, tiled=True)  10.5 us
    all_to_all x1, starting transfers between devices, local(): lax.all_to_all(partial.astype(jnp.bfloat16), 'dp', split_axis=0, concat_a...  3.79 us
  transfers between devices with their start and end apart: 3, of which 3 were waited for; matrix products, arithmetic and copies ran while one was open for 3% of the time, Pallas kernels for 0%

profile of v1, /device:TPU:0, one launch (start us, length us, event | category | flops | bytes accessed | tf_op | source)
XLA Modules:
  0.0 134.5 jit_solution(17641691783169842588)
XLA Ops:
  7.2 0.0 all-gather.3.cloned.1.call-start
  7.2 10.5 %all_to_all.21 = bf16[8,4,2048]{2,0,1:T(8,128)(2,1)} all-to-all(bf16[8,4,2048]{2,0,1:T(8,128)(2,1)} %bitcast.31), channel_id=1, replica_groups=mesh['dp'=4,'mp'=8] {'dp'}, dimensions={1} | all-to-all | bytes 262144 | tf_op jit(solution)/shard_map/all_to_all | solution.py:46
  17.7 22.3 %all-gather.3.cloned.1.call-done = bf16[4,64,2048]{2,1,0:T(8,128)(2,1)} async-done(((bf16[4,8,2048]{2,1,0:T(8,128)(2,1)}), bf16[4,64,2048]{2,1,0:T(8,128)(2,1)}) %all-gather.3.cloned.1.call-update) | async-done | bytes 1048592 | tf_op jit(solution)/shard_map/all_gather | solution.py:47
  40.0 11.9 %fusion.33 = (bf16[4,64,3584]{2,1,0:T(8,128)(2,1)}, f32[4,64,3584]{2,1,0:T(8,128)}) fusion(bf16[4,64,2048]{2,1,0:T(8,128)(2,1)} %all-gather.3.cloned.1.call-done, bf16[3584,2048]{1,0:T(8,128)(2,1)} %param.15), kind=kOutput, calls=%fused_computation.71 | convolution fusion | flops 3759013888 | bytes 21233664 | tf_op jit(solution)/shard_map/dot_general | solution.py:49
  51.9 3.8 %all-to-all-start.1 = ((bf16[4,64,3584]{2,1,0:T(8,128)(2,1)}), bf16[4,64,3584]{2,1,0:T(8,128)(2,1)S(1)}, u32[]{:S(2)}, u32[]{:S(2)}) async-start(bf16[4,64,3584]{2,1,0:T(8,128)(2,1)} %get-tuple-element.10), calls=%async_computation.1 | async-start | bytes 3670016 | tf_op jit(solution)/shard_map/all_to_all | solution.py:52
  55.7 0.2 reduce-window.7
  56.0 0.1 select_reduce_fusion.2
  56.1 0.4 fusion.36
  56.4 1.7 %fusion.37 = f32[8,64]{1,0:T(8,128)S(1)} fusion(bf16[8,8192]{1,0:T(8,128)(2,1)} %param.11, bf16[64,8192]{1,0:T(8,128)(2,1)} %param.16), kind=kOutput, calls=%fused_computation.75 | convolution fusion | flops 8388608 | bytes 1181696 | tf_op jit(solution)/shard_map/dot_general | solution.py:73
  58.1 1.6 %fusion.10 = f32[64,64]{1,0:T(8,128)S(1)} fusion(bf16[64,3584]{1,0:T(8,128)(2,1)} %param.18, bf16[64,3584]{1,0:T(8,128)(2,1)} %param.14, bf16[64,3584]{1,0:T(8,128)(2,1)S(1)} %copy-done.6), kind=kOutput, calls=%fused_computation.19 | convolution fusion | flops 31195136 | bytes 1392640 | tf_op jit(solution)/shard_map/dot_general | solution.py:69
  59.7 18.6 %all-to-all-done.1 = bf16[4,64,3584]{2,1,0:T(8,128)(2,1)S(1)} async-done(((bf16[4,64,3584]{2,1,0:T(8,128)(2,1)}), bf16[4,64,3584]{2,1,0:T(8,128)(2,1)S(1)}, u32[]{:S(2)}, u32[]{:S(2)}) %all-to-all-start.1) | async-done | bytes 1835040 | tf_op jit(solution)/shard_map/all_to_all | solution.py:52
  78.3 0.4 select_reduce_fusion
  78.8 1.9 %multiply_convert_fusion = (bf16[64,3584]{1,0:T(8,128)(2,1)S(1)}, bf16[64,3584]{1,0:T(8,128)(2,1)S(1)}) fusion(bf16[64,3584]{1,0:T(8,128)(2,1)} %param.13, f32[64,3584]{1,0:T(8,128)S(1)} %select_reduce_fusion, f32[4,64,3584]{2,1,0:T(8,128)} %get-tuple-element.11, s32[]{:T(128)S(6)} %select_n.74, bf16[64,3584]{1,0:T(8,128)(2,1)} %param.14), kind=kLoop, calls=%fused_computation.18 | loop fusion | flops 3670016 | bytes 3670020 | tf_op jit(solution)/shard_map/convert_element_type | solution.py:68
  80.8 0.3 fusion.35
  81.0 0.3 fusion.34
  81.3 0.7 pad_maximum_fusion
  82.1 29.4 %reduce-scatter.2.cloned.1.call-done = f32[8,192]{1,0:T(8,128)} async-done(((f32[64,192]{1,0:T(8,128)}), f32[8,192]{1,0:T(8,128)}) %reduce-scatter.2.cloned.1.call-update) | async-done | bytes 6160 | tf_op jit(solution)/shard_map/reduce_scatter | solution.py:75
  111.5 0.8 pad_maximum_fusion.1
  112.2 13.9 %all_gather.7 = f32[64,320]{1,0:T(8,128)S(1)} all-gather(f32[8,320]{1,0:T(8,128)S(1)} %pad_maximum_fusion.1), channel_id=1, replica_groups=mesh['dp'=4,'mp'=8] {'mp'}, dimensions={0}, use_global_device_ids=true | all-gather | bytes 92160 | tf_op jit(solution)/shard_map/all_gather | solution.py:76
  126.1 0.1 fusion.32
  126.2 0.1 slice.33
  126.3 0.3 convolution_select_fusion
  126.5 0.4 fusion.21
  127.0 0.6 fusion.14
  (25 shorter events, 0.1 us)
Async XLA Ops:
  7.2 48.9 %copy-start = (bf16[64,8192]{1,0:T(8,128)(2,1)S(1)}, bf16[64,8192]{1,0:T(8,128)(2,1)}, u32[]{:S(2)}) copy-start(bf16[64,8192]{1,0:T(8,128)(2,1)} %param.17) | copy-start | bytes 3145732
  7.2 32.8 %all-gather.3.cloned.1.call-start = ((), (), s32[]{:S(2)}) async-start(), calls=%async_computation.4 | async-start | bytes 1179648 | tf_op jit(solution)/shard_map/all_gather | solution.py:47
  51.9 3.8 %copy-start.7 = (s32[1,8]{1,0:T(1,128)S(1)}, s32[1,8]{1,0:T(1,128)}, u32[]{:S(2)}) copy-start(s32[1,8]{1,0:T(1,128)} %param.21) | copy-start | bytes 100
  51.9 4.1 %copy-start.3 = (bf16[8,8192]{1,0:T(8,128)(2,1)S(1)}, bf16[8,8192]{1,0:T(8,128)(2,1)}, u32[]{:S(2)}) copy-start(bf16[8,8192]{1,0:T(8,128)(2,1)} %param.12) | copy-start | bytes 393220
  51.9 6.2 %copy-start.6 = (bf16[64,3584]{1,0:T(8,128)(2,1)S(1)}, bf16[64,3584]{1,0:T(8,128)(2,1)}, u32[]{:S(2)}) copy-start(bf16[64,3584]{1,0:T(8,128)(2,1)} %param.13) | copy-start | bytes 1376260
  51.9 26.4 %all-to-all-start.1 = ((bf16[4,64,3584]{2,1,0:T(8,128)(2,1)}), bf16[4,64,3584]{2,1,0:T(8,128)(2,1)S(1)}, u32[]{:S(2)}, u32[]{:S(2)}) async-start(bf16[4,64,3584]{2,1,0:T(8,128)(2,1)} %get-tuple-element.10), calls=%async_computation.1 | async-start | bytes 3670016 | tf_op jit(solution)/shard_map/all_to_all | solution.py:52
  55.7 55.8 %reduce-scatter.2.cloned.1.call-start = ((), (), s32[]{:S(2)}) async-start(), calls=%async_computation.3 | async-start | bytes 73728 | tf_op jit(solution)/shard_map/reduce_scatter | solution.py:75
  59.7 21.1 %copy-start.4 = (bf16[64,3584]{1,0:T(8,128)(2,1)S(1)}, bf16[64,3584]{1,0:T(8,128)(2,1)}, u32[]{:S(2)}) copy-start(bf16[64,3584]{1,0:T(8,128)(2,1)} %param.20) | copy-start | bytes 1376260
  78.3 2.7 %copy-start.5 = (bf16[64,3584]{1,0:T(8,128)(2,1)S(1)}, bf16[64,3584]{1,0:T(8,128)(2,1)}, u32[]{:S(2)}) copy-start(bf16[64,3584]{1,0:T(8,128)(2,1)} %param.19) | copy-start | bytes 1376260
  80.7 46.9 %copy-start.1 = (bf16[64,3584]{1,0:T(8,128)(2,1)}, bf16[64,3584]{1,0:T(8,128)(2,1)S(1)}, u32[]{:S(2)}) copy-start(bf16[64,3584]{1,0:T(8,128)(2,1)S(1)} %get-tuple-element.5) | copy-start | bytes 1376260
  80.7 46.9 %copy-start.2 = (bf16[64,3584]{1,0:T(8,128)(2,1)}, bf16[64,3584]{1,0:T(8,128)(2,1)S(1)}, u32[]{:S(2)}) copy-start(bf16[64,3584]{1,0:T(8,128)(2,1)S(1)} %get-tuple-element.6) | copy-start | bytes 1376260
Sparse Core Ops, SparseCore 0:
  17.8 22.1 all-gather.2
  82.2 29.2 reduce-scatter.1

commit v2 on v0

v2 whole, which is shorter than its diff:
```python
import functools

import jax
import jax.numpy as jnp
from jax import lax
from jax.experimental import pallas as pl
from jax.experimental.pallas import tpu as pltpu
from jax.sharding import PartitionSpec as P

LANES = 128
F32 = jnp.float32
BF16 = jnp.bfloat16
NT = (((1,), (1,)), ((), ()))


def round_up(value, step):
    return -(-value // step) * step


def dot_nt(a, b):
    return lax.dot_general(a, b, NT, preferred_element_type=F32)


def kernel(
    n_dp,
    n_mp,
    chunk,
    hidden_in,
    out_grad,
    doc_sizes,
    gate_hbm,
    up_hbm,
    weight_hbm,
    proj_in_hbm,
    proj_grad_hbm,
    proj_hidden_hbm,
    proj_gate_hbm,
    proj_up_hbm,
    gate_grad,
    up_grad,
    sketches,
    gate_pre,
    up_pre,
    weight,
    proj_in,
    proj_grad,
    proj_hidden,
    proj_gate,
    proj_up,
    stage,
    lhs,
    own_part,
    send_part,
    recv_part,
    gate_factor,
    up_factor,
    stack,
    stack_in,
    sides,
    load_sem,
    weight_sem,
    own_sem,
    turn_send,
    turn_recv,
    row_send,
    row_recv,
    pair_send,
    pair_recv,
    part_send,
    part_recv,
    scatter_send,
    scatter_recv,
    gather_send,
    gather_recv,
):
    dp, mp = lax.axis_index("dp"), lax.axis_index("mp")
    pack, units = gate_pre.shape
    own_rows, features = out_grad.shape[0], weight.shape[1]
    rank = proj_in.shape[0]
    n_chunks = units // chunk
    n_row = n_mp // 2
    row, core = mp // 2, mp % 2
    mesh_id = pl.DeviceIdType.MESH

    def remote(src, dst, send, recv, device):
        return pltpu.make_async_remote_copy(
            src_ref=src, dst_ref=dst, send_sem=send, recv_sem=recv,
            device_id=device, device_id_type=mesh_id,
        )

    def dp_peer(k):
        return lax.rem(dp + k, n_dp)

    def dp_source(k):
        return lax.rem(dp + n_dp - k, n_dp)

    barrier = pltpu.get_barrier_semaphore()
    for k in range(1, n_dp):
        pl.semaphore_signal(barrier, inc=1, device_id=(dp_peer(k), mp), device_id_type=mesh_id)
    for k in range(1, n_mp):
        pl.semaphore_signal(
            barrier, inc=1, device_id=(dp, lax.rem(mp + k, n_mp)), device_id_type=mesh_id
        )

    own_columns = pl.ds(pl.multiple_of(dp * features, LANES), features)
    own_copy = pltpu.make_async_copy(out_grad.at[:, own_columns], stage.at[mp, dp], own_sem)
    own_copy.start()
    loads = [
        pltpu.make_async_copy(src, dst, load_sem.at[n])
        for n, (src, dst) in enumerate(
            [
                (gate_hbm, gate_pre),
                (up_hbm, up_pre),
                (proj_hidden_hbm, proj_hidden),
                (proj_grad_hbm, proj_grad),
                (proj_in_hbm, proj_in),
                (proj_gate_hbm, proj_gate),
                (proj_up_hbm, proj_up),
            ]
        )
    ]
    for load in loads:
        load.start()

    def weight_load(j):
        rows = pl.ds(pl.multiple_of(j * chunk, 16), chunk)
        return pltpu.make_async_copy(weight_hbm.at[rows], weight.at[rows], weight_sem.at[j])

    for j in range(n_chunks):
        weight_load(j).start()

    pl.semaphore_wait(barrier, n_dp - 1 + n_mp - 1)

    turns = []
    for k in range(1, n_dp):
        peer = dp_peer(k)
        columns = pl.ds(pl.multiple_of(peer * features, LANES), features)
        turn = remote(
            out_grad.at[:, columns], stage.at[mp, dp], turn_send.at[k - 1], turn_recv.at[k - 1],
            (peer, mp),
        )
        turn.start()
        turns.append(turn)
    own_copy.wait()
    for k in range(1, n_dp):
        landing = stage.at[mp, dp_source(k)]
        remote(landing, landing, turn_send.at[k - 1], turn_recv.at[k - 1], (dp, mp)).wait_recv()

    partner = (dp, row * 2 + (1 - core))
    sends = list(turns)
    mine = stage.at[mp]
    for k in range(1, n_row):
        copy = remote(
            mine, mine, row_send.at[k - 1], row_recv.at[k - 1],
            (dp, lax.rem(row + k, n_row) * 2 + core),
        )
        copy.start()
        sends.append(copy)
    copy = remote(mine, mine, pair_send.at[0], pair_recv.at[0], partner)
    copy.start()
    sends.append(copy)

    loads[0].wait()
    loads[1].wait()
    loads[2].wait()
    hidden_side = jnp.zeros((pack, rank), F32)
    for j in range(n_chunks):
        at = slice(j * chunk, (j + 1) * chunk)
        gate_value = gate_pre[:, at].astype(F32)
        up_value = up_pre[:, at].astype(F32)
        sigmoid_gate = 1.0 / (1.0 + jnp.exp(-gate_value))
        silu_gate = gate_value * sigmoid_gate
        hidden = (silu_gate * up_value).astype(BF16)
        gate_factor[j] = up_value * sigmoid_gate * (1.0 + gate_value * (1.0 - sigmoid_gate))
        up_factor[j] = silu_gate
        hidden_side = hidden_side + dot_nt(hidden, proj_hidden[:, at])
    stack[...] = jnp.zeros(stack.shape, F32)
    stack[:, :, 0:rank] = hidden_side.reshape(n_mp, own_rows, rank)
    loads[3].wait()
    grad_side = dot_nt(out_grad[...], proj_grad[...])
    loads[4].wait()
    input_side = dot_nt(hidden_in[...], proj_in[...])
    loads[5].wait()
    loads[6].wait()

    def assemble(source_row):
        for k in range(n_dp):
            owner = dp_peer(k)
            both = [stage[source_row * 2 + c, owner].astype(F32) for c in range(2)]
            at = pl.ds(pl.multiple_of(k * pack + source_row * 2 * own_rows, 16), 2 * own_rows)
            lhs[at, :] = jnp.concatenate(both, axis=0).astype(BF16)

    for k in range(1, n_row):
        source = lax.rem(row + n_row - k, n_row)
        landing = stage.at[source * 2 + core]
        remote(landing, landing, row_send.at[k - 1], row_recv.at[k - 1], (dp, mp)).wait_recv()
        copy = remote(landing, landing, pair_send.at[k], pair_recv.at[k], partner)
        copy.start()
        sends.append(copy)
    for k in range(n_row):
        source = lax.rem(row + n_row - k, n_row)
        landing = stage.at[source * 2 + (1 - core)]
        remote(landing, landing, pair_send.at[k], pair_recv.at[k], partner).wait_recv()
        assemble(source)

    def part_copy(j, k):
        return remote(
            send_part.at[j, k - 1], recv_part.at[j, k - 1], part_send.at[j, k - 1],
            part_recv.at[j, k - 1], (dp_peer(k), mp),
        )

    def multiply(j, carry):
        weight_load(j).wait()
        rows = pl.ds(pl.multiple_of(j * chunk, 16), chunk)
        part = dot_nt(lhs[...], weight[rows, :])
        for k in range(1, n_dp):
            send_part[j, k - 1] = part[k * pack : (k + 1) * pack].astype(BF16)
            part_copy(j, k).start()
        own_part[j] = part[:pack]
        return carry

    lax.fori_loop(0, n_chunks, multiply, 0)

    gate_side = jnp.zeros((pack, rank), F32)
    up_side = jnp.zeros((pack, rank), F32)
    for j in range(n_chunks):
        at = slice(j * chunk, (j + 1) * chunk)
        total = own_part[j]
        for k in range(1, n_dp):
            part_copy(j, k).wait_recv()
            total = total + recv_part[j, k - 1].astype(F32)
        gate_new = (total * gate_factor[j]).astype(BF16)
        up_new = (total * up_factor[j]).astype(BF16)
        gate_grad[:, at] = gate_new
        up_grad[:, at] = up_new
        gate_side = gate_side + dot_nt(gate_new, proj_gate[:, at])
        up_side = up_side + dot_nt(up_new, proj_up[:, at])
    stack[:, :, rank : 2 * rank] = gate_side.reshape(n_mp, own_rows, rank)
    stack[:, :, 2 * rank : 3 * rank] = up_side.reshape(n_mp, own_rows, rank)

    for k in range(1, n_mp):
        peer = lax.rem(mp + k, n_mp)
        copy = remote(
            stack.at[peer], stack_in.at[k - 1], scatter_send.at[k - 1], scatter_recv.at[k - 1],
            (dp, peer),
        )
        copy.start()
        sends.append(copy)
    own_sum = stack[mp]
    for k in range(1, n_mp):
        landing = stack_in.at[k - 1]
        remote(
            landing, landing, scatter_send.at[k - 1], scatter_recv.at[k - 1], (dp, mp)
        ).wait_recv()
        own_sum = own_sum + stack_in[k - 1]
    width = stack.shape[2]
    sides[mp] = jnp.zeros(sides.shape[1:], F32)
    sides[mp, :, :width] = own_sum
    sides[mp, :, 3 * rank : 4 * rank] = grad_side
    sides[mp, :, 4 * rank : 5 * rank] = input_side
    for k in range(1, n_mp):
        peer = lax.rem(mp + k, n_mp)
        copy = remote(
            sides.at[mp], sides.at[mp], gather_send.at[k - 1], gather_recv.at[k - 1], (dp, peer)
        )
        copy.start()
        sends.append(copy)

    row_count, docs = sketches.shape[1], doc_sizes.shape[1]
    rank_bits, doc_bits = rank.bit_length() - 1, docs.bit_length() - 1
    wide = sides.shape[2]

    def row_ids(columns):
        return mp * row_count + lax.broadcasted_iota(jnp.int32, (row_count, columns), 0)

    def which_of(ids):
        return lax.shift_right_logical(ids, rank_bits + doc_bits)

    ids = row_ids(wide)
    column = lax.broadcasted_iota(jnp.int32, ids.shape, 1)
    base = jnp.where(which_of(ids) == 0, 0, 4 * rank)
    pick = (column == base + (ids & (rank - 1))).astype(F32)
    ids = row_ids(pack)
    doc = lax.shift_right_logical(ids, rank_bits) & (docs - 1)
    start = jnp.zeros(ids.shape, jnp.int32)
    end = jnp.zeros(ids.shape, jnp.int32)
    passed = jnp.int32(0)
    for k in range(docs):
        after = passed + doc_sizes[0, k]
        start = jnp.where(doc == k, passed, start)
        end = jnp.where(doc == k, after, end)
        passed = after
    token = lax.broadcasted_iota(jnp.int32, ids.shape, 1)
    member = (token >= start) & (token < end)

    for k in range(1, n_mp):
        landing = sides.at[lax.rem(mp + n_mp - k, n_mp)]
        remote(
            landing, landing, gather_send.at[k - 1], gather_recv.at[k - 1], (dp, mp)
        ).wait_recv()
    full = sides[...].reshape(pack, wide)
    chosen = lax.dot_general(
        pick, full, NT, precision=lax.Precision.HIGHEST, preferred_element_type=F32
    )
    masked = jnp.where(member, chosen, 0.0)
    product = jnp.dot(
        masked, full, precision=lax.Precision.HIGHEST, preferred_element_type=F32
    )
    which = which_of(row_ids(rank))
    sketches[0] = jnp.where(
        which == 0,
        product[:, 3 * rank : 4 * rank],
        jnp.where(which == 1, product[:, rank : 2 * rank], product[:, 2 * rank : 3 * rank]),
    )

    for copy in sends:
        copy.wait_send()
    for j in range(n_chunks):
        for k in range(1, n_dp):
            part_copy(j, k).wait_send()


def local(
    hidden_in,
    out_grad,
    gate_pre,
    up_pre,
    down_weight,
    proj_in,
    proj_grad,
    proj_hidden,
    proj_gate,
    proj_up,
    doc_lengths,
):
    n_dp, n_mp = lax.axis_size("dp"), lax.axis_size("mp")
    own_rows, rank = hidden_in.shape[0], proj_in.shape[0]
    pack, units = gate_pre.shape
    features = down_weight.shape[1]
    docs = doc_lengths.shape[1]
    chunk = 4 * LANES
    if units % chunk:
        chunk = units
    n_chunks = units // chunk
    width, wide = round_up(3 * rank, LANES), round_up(5 * rank, LANES)
    dma = pltpu.SemaphoreType.DMA
    vmem = pl.BlockSpec(memory_space=pltpu.VMEM)
    far = pl.BlockSpec(memory_space=pl.ANY)
    return pl.pallas_call(
        functools.partial(kernel, n_dp, n_mp, chunk),
        out_shape=(
            jax.ShapeDtypeStruct((pack, units), BF16),
            jax.ShapeDtypeStruct((pack, units), BF16),
            jax.ShapeDtypeStruct((1, 3 * docs * rank // n_mp, rank), F32),
        ),
        in_specs=[vmem, vmem, pl.BlockSpec(memory_space=pltpu.SMEM)] + [far] * 8,
        out_specs=(vmem, vmem, vmem),
        scratch_shapes=[
            pltpu.VMEM((pack, units), BF16),
            pltpu.VMEM((pack, units), BF16),
            pltpu.VMEM((units, features), BF16),
            pltpu.VMEM(proj_in.shape, BF16),
            pltpu.VMEM(proj_grad.shape, BF16),
            pltpu.VMEM((rank, units), BF16),
            pltpu.VMEM((rank, units), BF16),
            pltpu.VMEM((rank, units), BF16),
            pltpu.VMEM((n_mp, n_dp, own_rows, features), BF16),
            pltpu.VMEM((n_dp * pack, features), BF16),
            pltpu.VMEM((n_chunks, pack, chunk), F32),
            pltpu.VMEM((n_chunks, n_dp - 1, pack, chunk), BF16),
            pltpu.VMEM((n_chunks, n_dp - 1, pack, chunk), BF16),
            pltpu.VMEM((n_chunks, pack, chunk), F32),
            pltpu.VMEM((n_chunks, pack, chunk), F32),
            pltpu.VMEM((n_mp, own_rows, width), F32),
            pltpu.VMEM((n_mp - 1, own_rows, width), F32),
            pltpu.VMEM((n_mp, own_rows, wide), F32),
            dma((7,)),
            dma((n_chunks,)),
            dma,
            dma((n_dp - 1,)),
            dma((n_dp - 1,)),
            dma((n_mp // 2 - 1,)),
            dma((n_mp // 2 - 1,)),
            dma((n_mp // 2,)),
            dma((n_mp // 2,)),
            dma((n_chunks, n_dp - 1)),
            dma((n_chunks, n_dp - 1)),
            dma((n_mp - 1,)),
            dma((n_mp - 1,)),
            dma((n_mp - 1,)),
            dma((n_mp - 1,)),
        ],
        compiler_params=pltpu.CompilerParams(
            collective_id=0, has_side_effects=True, vmem_limit_bytes=60 * 1024 * 1024
        ),
    )(
        hidden_in,
        out_grad,
        doc_lengths,
        gate_pre,
        up_pre,
        down_weight,
        proj_in,
        proj_grad,
        proj_hidden,
        proj_gate,
        proj_up,
    )


def solution(mesh):
    placed = (
        P(("dp", "mp"), None),
        P(("dp", "mp"), None),
        P("dp", "mp"),
        P("dp", "mp"),
        P("mp", "dp"),
        P(),
        P(),
        P(None, "mp"),
        P(None, "mp"),
        P(None, "mp"),
        P("dp", None),
    )
    return jax.shard_map(
        local,
        mesh=mesh,
        in_specs=placed,
        out_specs=(P("dp", "mp"), P("dp", "mp"), P("dp", "mp", None)),
        check_vma=False,
    )
```

time: 643 us -> 62.2 us (0.10)
  waiting for transfers between devices: 590 us -> 0 us
  Pallas kernels: 0 us -> 56.1 us
  matrix products: 32.3 us -> 0 us
  between operations: 13.9 us -> 0.64 us
    all_gather x2 -> x0, waiting for transfers between devices: 528 us -> none  [the longest x1 509 us: local(): weight_full = lax.all_gather(down_weight, 'dp', axis=1, tiled=True)]
    pallas_call x0 -> x1, Pallas kernels: none -> 56.1 us  [local(): pl.pallas_call(functools.partial(kernel, n_dp, n_mp, chunk), out_shape=(j...]
    dot_general x9 -> x0, matrix products: 32.3 us -> none  [the longest x1 24.7 us: local(): lax.dot_general(lax.all_gather(out_grad, 'mp', axis=0, tiled=True), weigh...]
    unnamed x5 -> x0, waiting for transfers between devices: 31.6 us -> none
    reduce_scatter x1 -> x0, waiting for transfers between devices: 30.5 us -> none  [local(): own_sides = lax.psum_scatter(stacked, 'mp', scatter_dimension=0, tiled=True)]
  transfers between devices with their start and end apart: 4 -> 0, of which waited for: 4 -> 0; matrix products, arithmetic and copies ran while one was open for 1% -> 0% of each run, Pallas kernels for 0% -> 0%
where the time goes in v2:
time: 62.2 us; the launch traced here: 61.9 us
  Pallas kernels  56.1 us (90%)
  local copies, waits for them, and re-layouts  5.23 us (8%)
  between operations  0.64 us (1%)
    pallas_call x1, Pallas kernels, local(): pl.pallas_call(functools.partial(kernel, n_dp, n_mp, chunk), out_shape=(j...  56.1 us
    unnamed x2, local copies, waits for them, and re-layouts  3.63 us
    pallas_call x1, local copies, waits for them, and re-layouts, local(): pl.pallas_call(functools.partial(kernel, n_dp, n_mp, chunk), out_shape=(j...  1.61 us

profile of v2, /device:TPU:0, one launch (start us, length us, event | category | flops | bytes accessed | tf_op | source)
XLA Modules:
  0.0 61.9 jit_solution(10333539145238985355)
XLA Ops:
  0.6 56.1 %shard_map.130 = (bf16[64,3584]{1,0:T(8,128)(2,1)}, bf16[64,3584]{1,0:T(8,128)(2,1)}, f32[1,192,64]{2,1,0:T(8,128)}) custom-call(bf16[8,8192]{1,0:T(8,128)(2,1)} %hidden_in.1, bf16[8,8192]{1,0:T(8,128)(2,1)} %out_grad.1, s32[1,8]{1,0:T(1,128)} %doc_sizes.1, bf16[64,3584]{1,0:T(8,128)(2,1)} %gate_hbm.1, bf16[64,3584]{1,0:T(8,128)(2,1)} %up_hbm.1, ...), custom_call_target="tpu_custom_call" | custom-call | tf_op jit(solution)/shard_map/pallas_call | solution.py:349
  56.7 1.6 %copy.14 = f32[1,192,64]{1,2,0:T(8,128)} copy(f32[1,192,64]{2,1,0:T(8,128)} %get-tuple-element.5) | data formatting | bytes 98304 | tf_op jit(solution)/shard_map/pallas_call | solution.py:349
  58.3 1.8 %copy.17 = bf16[64,3584]{1,0:T(8,128)(2,1)} copy(bf16[64,3584]{1,0:T(8,128)(2,1)} %get-tuple-element.9) | data formatting | bytes 917504
  60.1 1.8 %copy.18 = bf16[64,3584]{1,0:T(8,128)(2,1)} copy(bf16[64,3584]{1,0:T(8,128)(2,1)} %get-tuple-element.10) | data formatting | bytes 917504

commit v3 on v2

v3 whole, which is shorter than its diff:
```python
import functools

import jax
import jax.numpy as jnp
from jax import lax
from jax.experimental import pallas as pl
from jax.experimental.pallas import tpu as pltpu
from jax.sharding import PartitionSpec as P

LANES = 128
F32 = jnp.float32
BF16 = jnp.bfloat16
NT = (((1,), (1,)), ((), ()))


def dot_nt(a, b):
    return lax.dot_general(a, b, NT, preferred_element_type=F32)


def kernel(
    n_dp,
    n_mp,
    chunk,
    hidden_in,
    out_grad,
    doc_sizes,
    gate_hbm,
    up_hbm,
    weight_hbm,
    proj_in_hbm,
    proj_grad_hbm,
    proj_hidden_hbm,
    proj_gate_hbm,
    proj_up_hbm,
    gate_grad,
    up_grad,
    sketches,
    gate_pre,
    up_pre,
    weight,
    proj_in,
    proj_grad,
    proj_hidden,
    proj_gate,
    proj_up,
    stage,
    lhs,
    own_part,
    send_part,
    recv_part,
    gate_factor,
    up_factor,
    side_part,
    side_in,
    side_sum,
    row_sides,
    masked,
    load_sem,
    weight_sem,
    own_sem,
    turn_send,
    turn_recv,
    row_send,
    row_recv,
    pair_send,
    pair_recv,
    part_send,
    part_recv,
    side_send,
    side_recv,
    gather_send,
    gather_recv,
):
    dp, mp = lax.axis_index("dp"), lax.axis_index("mp")
    pack, units = gate_pre.shape
    own_rows, features = out_grad.shape[0], weight.shape[1]
    rank = proj_in.shape[0]
    n_chunks = units // chunk
    n_row = n_mp // 2
    row, core = mp // 2, mp % 2
    half = n_row // 2
    half_pack = pack // 2
    row_count, docs = sketches.shape[1], doc_sizes.shape[1]
    rank_bits, doc_bits = rank.bit_length() - 1, docs.bit_length() - 1
    mesh_id = pl.DeviceIdType.MESH

    def remote(src, dst, send, recv, device):
        return pltpu.make_async_remote_copy(
            src_ref=src, dst_ref=dst, send_sem=send, recv_sem=recv,
            device_id=device, device_id_type=mesh_id,
        )

    def dp_peer(k):
        return lax.rem(dp + k, n_dp)

    def dp_source(k):
        return lax.rem(dp + n_dp - k, n_dp)

    def half_of(g):
        return row // half if g == 0 else 1 - row // half

    def row_peer(k):
        return half_of(k // half) * half + lax.rem(row % half + k % half, half)

    def row_source(k):
        return half_of(k // half) * half + lax.rem(row % half + half - k % half, half)

    def needs(device, w):
        block = docs * rank
        return (device * row_count < (w + 1) * block) & ((device + 1) * row_count > w * block)

    barrier = pltpu.get_barrier_semaphore()
    for k in range(1, n_dp):
        pl.semaphore_signal(barrier, inc=1, device_id=(dp_peer(k), mp), device_id_type=mesh_id)
    for k in range(1, n_mp):
        pl.semaphore_signal(
            barrier, inc=1, device_id=(dp, lax.rem(mp + k, n_mp)), device_id_type=mesh_id
        )

    own_columns = pl.ds(pl.multiple_of(dp * features, LANES), features)
    own_copy = pltpu.make_async_copy(out_grad.at[:, own_columns], stage.at[mp, dp], own_sem)
    own_copy.start()
    loads = [
        pltpu.make_async_copy(src, dst, load_sem.at[n])
        for n, (src, dst) in enumerate(
            [
                (gate_hbm, gate_pre),
                (up_hbm, up_pre),
                (proj_hidden_hbm, proj_hidden),
                (proj_grad_hbm, proj_grad),
                (proj_in_hbm, proj_in),
                (proj_gate_hbm, proj_gate),
                (proj_up_hbm, proj_up),
            ]
        )
    ]
    for load in loads:
        load.start()

    def weight_load(j):
        rows = pl.ds(pl.multiple_of(j * chunk, 16), chunk)
        return pltpu.make_async_copy(weight_hbm.at[rows], weight.at[rows], weight_sem.at[j])

    for j in range(n_chunks):
        weight_load(j).start()

    pl.semaphore_wait(barrier, n_dp - 1 + n_mp - 1)

    turns = []
    for k in range(1, n_dp):
        peer = dp_peer(k)
        columns = pl.ds(pl.multiple_of(peer * features, LANES), features)
        turn = remote(
            out_grad.at[:, columns], stage.at[mp, dp], turn_send.at[k - 1], turn_recv.at[k - 1],
            (peer, mp),
        )
        turn.start()
        turns.append(turn)
    own_copy.wait()
    for k in range(1, n_dp):
        landing = stage.at[mp, dp_source(k)]
        remote(landing, landing, turn_send.at[k - 1], turn_recv.at[k - 1], (dp, mp)).wait_recv()

    partner = (dp, row * 2 + (1 - core))
    sends = list(turns)
    mine = stage.at[mp]
    copy = remote(mine, mine, pair_send.at[0], pair_recv.at[0], partner)
    copy.start()
    sends.append(copy)
    for k in range(1, n_row):
        copy = remote(
            mine, mine, row_send.at[k - 1], row_recv.at[k - 1], (dp, row_peer(k) * 2 + core)
        )
        copy.start()
        sends.append(copy)

    loads[0].wait()
    loads[1].wait()
    loads[2].wait()
    hidden_side = jnp.zeros((pack, rank), F32)
    for j in range(n_chunks):
        at = slice(j * chunk, (j + 1) * chunk)
        gate_value = gate_pre[:, at].astype(F32)
        up_value = up_pre[:, at].astype(F32)
        sigmoid_gate = 1.0 / (1.0 + jnp.exp(-gate_value))
        silu_gate = gate_value * sigmoid_gate
        hidden = (silu_gate * up_value).astype(BF16)
        gate_factor[j] = up_value * sigmoid_gate * (1.0 + gate_value * (1.0 - sigmoid_gate))
        up_factor[j] = silu_gate
        hidden_side = hidden_side + dot_nt(hidden, proj_hidden[:, at])

    def side_copy(w, k):
        peer = lax.rem(mp + k, n_mp)
        return remote(
            side_part.at[w], side_in.at[w, k - 1], side_send.at[w, k - 1],
            side_recv.at[w, k - 1], (dp, peer),
        )

    def send_side(w, value):
        side_part[w, :, :rank] = value[:half_pack]
        side_part[w, :, rank:] = value[half_pack:]
        for k in range(1, n_mp):
            @pl.when(needs(lax.rem(mp + k, n_mp), w))
            def _():
                side_copy(w, k).start()

    def sum_side(w):
        @pl.when(needs(mp, w))
        def _():
            value = side_part[w]
            for k in range(1, n_mp):
                side_copy(w, k).wait_recv()
                value = value + side_in[w, k - 1]
            side_sum[w, :half_pack] = value[:, :rank]
            side_sum[w, half_pack:] = value[:, rank:]

    side_sum[...] = jnp.zeros(side_sum.shape, F32)
    send_side(0, hidden_side)

    def assemble(g, source_row):
        for k in range(n_dp):
            owner = dp_peer(k)
            both = [stage[source_row * 2 + c, owner].astype(F32) for c in range(2)]
            at = pl.ds(
                pl.multiple_of(k * half_pack + (source_row % half) * 2 * own_rows, 16),
                2 * own_rows,
            )
            lhs[g, at, :] = jnp.concatenate(both, axis=0).astype(BF16)

    def part_copy(g, j, k):
        return remote(
            send_part.at[g, j, k - 1], recv_part.at[g, j, k - 1], part_send.at[g, j, k - 1],
            part_recv.at[g, j, k - 1], (dp_peer(k), mp),
        )

    def half_step(g):
        for k in range(g * half, (g + 1) * half):
            if k == 0:
                continue
            landing = stage.at[row_source(k) * 2 + core]
            remote(landing, landing, row_send.at[k - 1], row_recv.at[k - 1], partner).wait_recv()
            copy = remote(landing, landing, pair_send.at[k], pair_recv.at[k], partner)
            copy.start()
            sends.append(copy)
        for k in range(g * half, (g + 1) * half):
            landing = stage.at[row_source(k) * 2 + (1 - core)]
            remote(landing, landing, pair_send.at[k], pair_recv.at[k], partner).wait_recv()
            assemble(g, row_source(k))

        def multiply(j, carry):
            if g == 0:
                weight_load(j).wait()
            rows = pl.ds(pl.multiple_of(j * chunk, 16), chunk)
            part = dot_nt(lhs[g], weight[rows, :])
            for k in range(1, n_dp):
                send_part[g, j, k - 1] = part[k * half_pack : (k + 1) * half_pack].astype(BF16)
                part_copy(g, j, k).start()
            own_part[g, j] = part[:half_pack]
            return carry

        lax.fori_loop(0, n_chunks, multiply, 0)

    half_step(0)
    loads[3].wait()
    row_sides[mp, :, :rank] = dot_nt(out_grad[...], proj_grad[...])
    loads[4].wait()
    row_sides[mp, :, rank:] = dot_nt(hidden_in[...], proj_in[...])
    for k in range(1, n_mp):
        mine = row_sides.at[mp]
        copy = remote(
            mine, mine, gather_send.at[k - 1], gather_recv.at[k - 1], (dp, lax.rem(mp + k, n_mp))
        )
        copy.start()
        sends.append(copy)
    loads[5].wait()
    loads[6].wait()
    half_step(1)

    def row_ids(columns):
        return mp * row_count + lax.broadcasted_iota(jnp.int32, (row_count, columns), 0)

    def which_of(ids):
        return lax.shift_right_logical(ids, rank_bits + doc_bits)

    def precise(a, b, dims):
        return lax.dot_general(
            a, b, dims, precision=lax.Precision.HIGHEST, preferred_element_type=F32
        )

    ids = row_ids(rank)
    which = which_of(ids)
    column = lax.broadcasted_iota(jnp.int32, ids.shape, 1)
    pick = (column == (ids & (rank - 1))).astype(F32)
    ids = row_ids(pack)
    doc = lax.shift_right_logical(ids, rank_bits) & (docs - 1)
    start = jnp.zeros(ids.shape, jnp.int32)
    end = jnp.zeros(ids.shape, jnp.int32)
    passed = jnp.int32(0)
    for k in range(docs):
        after = passed + doc_sizes[0, k]
        start = jnp.where(doc == k, passed, start)
        end = jnp.where(doc == k, after, end)
        passed = after
    token = lax.broadcasted_iota(jnp.int32, ids.shape, 1)
    for k in range(1, n_mp):
        landing = row_sides.at[lax.rem(mp + n_mp - k, n_mp)]
        remote(landing, landing, gather_send.at[k - 1], gather_recv.at[k - 1], partner).wait_recv()
    sum_side(0)
    by_row = row_sides[...].reshape(pack, 2 * rank)
    chosen = jnp.where(
        which_of(ids) == 0,
        precise(pick, side_sum[0], NT),
        precise(pick, by_row[:, rank:], NT),
    )
    masked[...] = jnp.where((token >= start) & (token < end), chosen, 0.0)
    plain = (((1,), (0,)), ((), ()))
    sketches[0] = precise(masked[...], by_row[:, :rank], plain)

    gate_side = jnp.zeros((pack, rank), F32)
    up_side = jnp.zeros((pack, rank), F32)
    for j in range(n_chunks):
        at = slice(j * chunk, (j + 1) * chunk)
        for g in range(2):
            total = own_part[g, j]
            for k in range(1, n_dp):
                part_copy(g, j, k).wait_recv()
                total = total + recv_part[g, j, k - 1].astype(F32)
            tokens = pl.ds(pl.multiple_of(half_of(g) * half_pack, 16), half_pack)
            gate_grad[tokens, at] = (total * gate_factor[j, tokens, :]).astype(BF16)
            up_grad[tokens, at] = (total * up_factor[j, tokens, :]).astype(BF16)
        gate_side = gate_side + dot_nt(gate_grad[:, at], proj_gate[:, at])
        up_side = up_side + dot_nt(up_grad[:, at], proj_up[:, at])
    send_side(1, gate_side)
    send_side(2, up_side)
    for w in (1, 2):
        sum_side(w)

        @pl.when(needs(mp, w))
        def _():
            product = precise(masked[...], side_sum[w], plain)
            sketches[0] = jnp.where(which_of(row_ids(rank)) == w, product, sketches[0])

    for w in range(3):
        for k in range(1, n_mp):
            @pl.when(needs(lax.rem(mp + k, n_mp), w))
            def _():
                side_copy(w, k).wait_send()
    for copy in sends:
        copy.wait_send()
    for g in range(2):
        for j in range(n_chunks):
            for k in range(1, n_dp):
                part_copy(g, j, k).wait_send()


def flush(*refs):
    for src, dst in zip(refs[:3], refs[3:]):
        dst[...] = src[...]


def local(
    hidden_in,
    out_grad,
    gate_pre,
    up_pre,
    down_weight,
    proj_in,
    proj_grad,
    proj_hidden,
    proj_gate,
    proj_up,
    doc_lengths,
):
    n_dp, n_mp = lax.axis_size("dp"), lax.axis_size("mp")
    own_rows, rank = hidden_in.shape[0], proj_in.shape[0]
    pack, units = gate_pre.shape
    features = down_weight.shape[1]
    docs = doc_lengths.shape[1]
    chunk = 4 * LANES
    if units % chunk:
        chunk = units
    n_chunks = units // chunk
    row_count = 3 * docs * rank // n_mp
    dma = pltpu.SemaphoreType.DMA
    vmem = pl.BlockSpec(memory_space=pltpu.VMEM)
    far = pl.BlockSpec(memory_space=pl.ANY)
    shapes = (
        jax.ShapeDtypeStruct((pack, units), BF16),
        jax.ShapeDtypeStruct((pack, units), BF16),
        jax.ShapeDtypeStruct((1, row_count, rank), F32),
    )
    results = pl.pallas_call(
        functools.partial(kernel, n_dp, n_mp, chunk),
        out_shape=shapes,
        in_specs=[vmem, vmem, pl.BlockSpec(memory_space=pltpu.SMEM)] + [far] * 8,
        out_specs=(vmem, vmem, vmem),
        scratch_shapes=[
            pltpu.VMEM((pack, units), BF16),
            pltpu.VMEM((pack, units), BF16),
            pltpu.VMEM((units, features), BF16),
            pltpu.VMEM(proj_in.shape, BF16),
            pltpu.VMEM(proj_grad.shape, BF16),
            pltpu.VMEM((rank, units), BF16),
            pltpu.VMEM((rank, units), BF16),
            pltpu.VMEM((rank, units), BF16),
            pltpu.VMEM((n_mp, n_dp, own_rows, features), BF16),
            pltpu.VMEM((2, n_dp * pack // 2, features), BF16),
            pltpu.VMEM((2, n_chunks, pack // 2, chunk), F32),
            pltpu.VMEM((2, n_chunks, n_dp - 1, pack // 2, chunk), BF16),
            pltpu.VMEM((2, n_chunks, n_dp - 1, pack // 2, chunk), BF16),
            pltpu.VMEM((n_chunks, pack, chunk), F32),
            pltpu.VMEM((n_chunks, pack, chunk), F32),
            pltpu.VMEM((3, pack // 2, 2 * rank), F32),
            pltpu.VMEM((3, n_mp - 1, pack // 2, 2 * rank), F32),
            pltpu.VMEM((3, pack, rank), F32),
            pltpu.VMEM((n_mp, own_rows, 2 * rank), F32),
            pltpu.VMEM((row_count, pack), F32),
            dma((7,)),
            dma((n_chunks,)),
            dma,
            dma((n_dp - 1,)),
            dma((n_dp - 1,)),
            dma((n_mp // 2 - 1,)),
            dma((n_mp // 2 - 1,)),
            dma((n_mp // 2,)),
            dma((n_mp // 2,)),
            dma((2, n_chunks, n_dp - 1)),
            dma((2, n_chunks, n_dp - 1)),
            dma((3, n_mp - 1)),
            dma((3, n_mp - 1)),
            dma((n_mp - 1,)),
            dma((n_mp - 1,)),
        ],
        compiler_params=pltpu.CompilerParams(
            collective_id=0, has_side_effects=True, vmem_limit_bytes=60 * 1024 * 1024
        ),
    )(
        hidden_in,
        out_grad,
        doc_lengths,
        gate_pre,
        up_pre,
        down_weight,
        proj_in,
        proj_grad,
        proj_hidden,
        proj_gate,
        proj_up,
    )
    return pl.pallas_call(
        flush, out_shape=shapes, in_specs=[vmem] * 3, out_specs=(vmem,) * 3
    )(*results)


def solution(mesh):
    placed = (
        P(("dp", "mp"), None),
        P(("dp", "mp"), None),
        P("dp", "mp"),
        P("dp", "mp"),
        P("mp", "dp"),
        P(),
        P(),
        P(None, "mp"),
        P(None, "mp"),
        P(None, "mp"),
        P("dp", None),
    )
    return jax.shard_map(
        local,
        mesh=mesh,
        in_specs=placed,
        out_specs=(P("dp", "mp"), P("dp", "mp"), P("dp", "mp", None)),
        check_vma=False,
    )
```

time: 62.2 us -> 51.3 us (0.82)
  Pallas kernels: 56.1 us -> 48.8 us
  local copies, waits for them, and re-layouts: 5.23 us -> 1.6 us
    pallas_call x1 -> x2, Pallas kernels: 56.1 us -> 48.8 us  [the longest x1 46.7 us: local(): pl.pallas_call(functools.partial(kernel, n_dp, n_mp, chunk), out_shape=sh...]
    unnamed x2 -> x0, local copies, waits for them, and re-layouts: 3.63 us -> none
where the time goes in v3:
time: 51.3 us; the launch traced here: 51.1 us
  Pallas kernels  48.8 us (95%)
  local copies, waits for them, and re-layouts  1.6 us (3%)
  between operations  0.64 us (1%)
    pallas_call x1, Pallas kernels, local(): pl.pallas_call(functools.partial(kernel, n_dp, n_mp, chunk), out_shape=sh...  46.7 us
    pallas_call x1, Pallas kernels, local(): pl.pallas_call(flush, out_shape=shapes, in_specs=[vmem] * 3, out_specs=(v...  2.15 us
    pallas_call x1, local copies, waits for them, and re-layouts, local(): pl.pallas_call(flush, out_shape=shapes, in_specs=[vmem] * 3, out_specs=(v...  1.6 us

profile of v3, /device:TPU:0, one launch (start us, length us, event | category | flops | bytes accessed | tf_op | source)
XLA Modules:
  0.0 51.1 jit_solution(7917513948929312207)
XLA Ops:
  0.6 46.7 %shard_map.130 = (bf16[64,3584]{1,0:T(8,128)(2,1)}, bf16[64,3584]{1,0:T(8,128)(2,1)}, f32[1,192,64]{2,1,0:T(8,128)}) custom-call(bf16[8,8192]{1,0:T(8,128)(2,1)} %hidden_in.1, bf16[8,8192]{1,0:T(8,128)(2,1)} %out_grad.1, s32[1,8]{1,0:T(1,128)} %doc_sizes.1, bf16[64,3584]{1,0:T(8,128)(2,1)} %gate_hbm.1, bf16[64,3584]{1,0:T(8,128)(2,1)} %up_hbm.1, ...), custom_call_target="tpu_custom_call" | custom-call | tf_op jit(solution)/shard_map/pallas_call | solution.py:392
  47.3 2.1 %shard_map.131 = (bf16[64,3584]{1,0:T(8,128)(2,1)}, bf16[64,3584]{1,0:T(8,128)(2,1)}, f32[1,192,64]{2,1,0:T(8,128)}) custom-call(bf16[64,3584]{1,0:T(8,128)(2,1)} %get-tuple-element.6.refs_0_, bf16[64,3584]{1,0:T(8,128)(2,1)} %get-tuple-element.7.refs_1_, f32[1,192,64]{2,1,0:T(8,128)} %get-tuple-element.8.refs_2_), custom_call_target="tpu_custom_call" | custom-call | tf_op jit(solution)/shard_map/pallas_call | solution.py:450
  49.4 1.6 %copy.14 = f32[1,192,64]{1,2,0:T(8,128)} copy(f32[1,192,64]{2,1,0:T(8,128)} %get-tuple-element.11) | data formatting | bytes 98304 | tf_op jit(solution)/shard_map/pallas_call | solution.py:450

commit v4 on v3

--- a/solution.py
+++ b/solution.py
@@ -261,6 +261,7 @@
         lax.fori_loop(0, n_chunks, multiply, 0)
 
     half_step(0)
+    half_step(1)
     loads[3].wait()
     row_sides[mp, :, :rank] = dot_nt(out_grad[...], proj_grad[...])
     loads[4].wait()
@@ -274,7 +275,6 @@
         sends.append(copy)
     loads[5].wait()
     loads[6].wait()
-    half_step(1)
 
     def row_ids(columns):
         return mp * row_count + lax.broadcasted_iota(jnp.int32, (row_count, columns), 0)
@@ -354,8 +354,9 @@
 
 
 def flush(*refs):
-    for src, dst in zip(refs[:3], refs[3:]):
+    for src, dst in zip(refs[:2], refs[3:5]):
         dst[...] = src[...]
+    refs[5][0] = refs[2][0].T
 
 
 def local(
@@ -447,9 +448,11 @@
         proj_gate,
         proj_up,
     )
-    return pl.pallas_call(
-        flush, out_shape=shapes, in_specs=[vmem] * 3, out_specs=(vmem,) * 3
+    turned = jax.ShapeDtypeStruct((1, rank, row_count), F32)
+    gate_grad, up_grad, sketches = pl.pallas_call(
+        flush, out_shape=shapes[:2] + (turned,), in_specs=[vmem] * 3, out_specs=(vmem,) * 3
     )(*results)
+    return gate_grad, up_grad, jnp.swapaxes(sketches, 1, 2)
 
 
 def solution(mesh):

time: 51.3 us -> 49.7 us (0.969)
  local copies, waits for them, and re-layouts: 1.6 us -> 0 us
    pallas_call x1 -> x0, local copies, waits for them, and re-layouts: 1.6 us -> none  [local(): pl.pallas_call(flush, out_shape=shapes, in_specs=[vmem] * 3, out_specs=(v...]
where the time goes in v4:
time: 49.7 us; the launch traced here: 49.4 us
  Pallas kernels  48.8 us (98%)
  between operations  0.64 us (1%)
    pallas_call x1, Pallas kernels, local(): pl.pallas_call(functools.partial(kernel, n_dp, n_mp, chunk), out_shape=sh...  46.7 us
    pallas_call x1, Pallas kernels, local(): pl.pallas_call(flush, out_shape=shapes[:2] + (turned,), in_specs=[vmem] *...  2.14 us

profile of v4, /device:TPU:0, one launch (start us, length us, event | category | flops | bytes accessed | tf_op | source)
XLA Modules:
  0.0 49.4 jit_solution(16525458968276744848)
XLA Ops:
  0.6 46.7 %shard_map.130 = (bf16[64,3584]{1,0:T(8,128)(2,1)}, bf16[64,3584]{1,0:T(8,128)(2,1)}, f32[1,192,64]{2,1,0:T(8,128)}) custom-call(bf16[8,8192]{1,0:T(8,128)(2,1)} %hidden_in.1, bf16[8,8192]{1,0:T(8,128)(2,1)} %out_grad.1, s32[1,8]{1,0:T(1,128)} %doc_sizes.1, bf16[64,3584]{1,0:T(8,128)(2,1)} %gate_hbm.1, bf16[64,3584]{1,0:T(8,128)(2,1)} %up_hbm.1, ...), custom_call_target="tpu_custom_call" | custom-call | tf_op jit(solution)/shard_map/pallas_call | solution.py:393
  47.3 2.1 %shard_map.131 = (bf16[64,3584]{1,0:T(8,128)(2,1)}, bf16[64,3584]{1,0:T(8,128)(2,1)}, f32[1,64,192]{2,1,0:T(8,128)}) custom-call(bf16[64,3584]{1,0:T(8,128)(2,1)} %get-tuple-element.9.refs_0_, bf16[64,3584]{1,0:T(8,128)(2,1)} %get-tuple-element.10.refs_1_, f32[1,192,64]{2,1,0:T(8,128)} %get-tuple-element.11.refs_2_), custom_call_target="tpu_custom_call" | custom-call | tf_op jit(solution)/shard_map/pallas_call | solution.py:452
